TPU v7x, 32 devices: a whole 2x2x4 slice. The times are simulated.
32 devices in a mesh: dp: 8 (over y, x, core), tensor: 4 (over z).
Axes of the slice: x: 2, y: 2, z: 4, core: 2. Of those that a mesh axis runs over, the one named last changes fastest.
Arguments:
- activations: bfloat16 [8192, 1024], P(('dp', 'tensor')), may hold values from -6 to 6
- segments: int32 [8192], P('dp'), may hold values from 0 to 31, as said below
- attn_weight: bfloat16 [1, 3, 1024, 1024], P(None, None, 'dp', 'tensor'), may hold values from -0.1875 to 0.1875
- out_weight: bfloat16 [1, 1024, 1024], P(None, 'tensor', 'dp'), may hold values from -0.75 to 0.75
- up_weight: bfloat16 [1, 1024, 4096], P(None, 'dp', 'tensor'), may hold values from -0.1875 to 0.1875
- down_weight: bfloat16 [1, 4096, 1024], P(None, 'tensor', 'dp'), may hold values from -0.09375 to 0.09375
- norm_gains: bfloat16 [1, 2, 1024], P(None, None, 'dp'), may hold values from 0.5 to 1.5
- bias_rows: bfloat16 [1, 10, 1024], P(None, None, 'dp'), may hold values from -1 to 1
- cotangent: float32 [8192, 1024], P(('dp', 'tensor')), may hold values from -6 to 6
Outputs:
- layer_output: float32 [8192, 1024], P(('dp', 'tensor'))
- input_grad: float32 [8192, 1024], P(('dp', 'tensor'))
- attn_weight_grad: float32 [1, 3, 1024, 1024], P(None, None, 'dp', 'tensor')
- out_weight_grad: float32 [1, 1024, 1024], P(None, 'tensor', 'dp')
- up_weight_grad: float32 [1, 1024, 4096], P(None, 'dp', 'tensor')
- down_weight_grad: float32 [1, 4096, 1024], P(None, 'tensor', 'dp')
- gain_grad: float32 [1, 2, 1024], P(None, None, 'dp')
- bias_grad: float32 [1, 10, 1024], P(None, None, 'dp')
Inputs may be any that keep to these rules, and one draw needn't show every extreme that they name: `segments`: within each sequence of 1024 tokens ids never fall; every document has 200 tokens or more; sequences share no id; the last document of sequence j has id 4 j + 3 and ids of sequence j lie in 4 j to 4 j + 3.
All inputs are finite; a program needn't handle non-finite values.
Results may differ from a plain program's by a relative error of at most 0.018.
Values may be sent and summed in bfloat16 or wider, within the bound.
A program may use at most 128 MiB of HBM per device.

v0:
```python
import jax
import jax.numpy as jnp
from jax import lax
from jax.sharding import PartitionSpec as P

HD = 64
SEQ = 1024


EPSILON = 1e-05
MASKED = -1e30


def layer_norm(values, gain_row, shift_row):
    center = values - jnp.mean(values, axis=-1, keepdims=True)
    spread = jnp.mean(center * center, axis=-1, keepdims=True)
    return center * lax.rsqrt(spread + EPSILON) * gain_row + shift_row


def gelu_tanh(values):
    return jax.nn.gelu(values, approximate=True)


def visible_mask(segments, first_row, seq_start, block_rows):
    query_pos = first_row + jnp.arange(block_rows)
    key_pos = seq_start + jnp.arange(SEQ)
    query_seg = lax.dynamic_slice_in_dim(segments, first_row, block_rows, 0)
    return (key_pos[None, :] <= query_pos[:, None]) & (query_seg[:, None] == segments[None, :])


def block_scores(project, segments, first_row, block_rows):
    head_count = project.shape[2] // HD
    seq_start = first_row // SEQ * SEQ
    query_rows = lax.dynamic_slice_in_dim(project, first_row, block_rows, 0)[:, 0].reshape(
        block_rows, head_count, HD
    )
    key_vecs = project[:, 1].reshape(SEQ, head_count, HD)
    value_vecs = project[:, 2].reshape(SEQ, head_count, HD)
    scores = jnp.einsum(
        "qhd,khd->hqk", query_rows, key_vecs, preferred_element_type=jnp.float32
    ) * HD ** (-0.5)
    visible = visible_mask(segments, first_row, seq_start, block_rows)
    scores = jnp.where(visible[None], scores, MASKED)
    return (query_rows, key_vecs, value_vecs, scores)


def attend(project, segments):
    token_count = project.shape[0]
    block_rows = min(512, SEQ)

    def attend_one_block(block_index):
        first_row = block_index * block_rows
        query_rows, key_vecs, value_vecs, scores = block_scores(
            project, segments, first_row, block_rows
        )
        row_max = jnp.max(scores, axis=-1, keepdims=True)
        raised = jnp.exp(scores - row_max)
        row_total = jnp.sum(raised, axis=-1, keepdims=True)
        prob_rows = (raised / row_total).astype(jnp.bfloat16)
        attended = jnp.einsum(
            "hqk,khd->qhd", prob_rows, value_vecs, preferred_element_type=jnp.float32
        )
        return (
            attended.reshape(block_rows, -1).astype(jnp.bfloat16),
            (row_max + jnp.log(row_total))[:, :, 0],
        )

    attended, log_total = lax.map(attend_one_block, jnp.arange(token_count // block_rows))
    return (attended.reshape(token_count, -1), log_total)


def attend_back(project, segments, log_total, attended_grad):
    token_count = project.shape[0]
    head_width = project.shape[2]
    head_count = head_width // HD
    block_rows = min(512, SEQ)
    per_seq = SEQ // block_rows
    factor = HD ** (-0.5)

    def one_sequence(seq_index):

        def one_one_block(totals, local_index):
            key_total, value_total = totals
            block_index = seq_index * per_seq + local_index
            first_row = block_index * block_rows
            query_rows, key_vecs, value_vecs, scores = block_scores(
                project, segments, first_row, block_rows
            )
            prob_rows = jnp.exp(scores - log_total[block_index][:, :, None])
            grad_rows = lax.dynamic_slice_in_dim(attended_grad, first_row, block_rows, 0).reshape(
                block_rows, head_count, HD
            )
            prob_grad = jnp.einsum(
                "qhd,khd->hqk", grad_rows, value_vecs, preferred_element_type=jnp.float32
            )
            inner_sum = jnp.sum(prob_rows * prob_grad, axis=-1, keepdims=True)
            score_grad = (prob_rows * (prob_grad - inner_sum)).astype(jnp.bfloat16)
            query_grad = (
                jnp.einsum("hqk,khd->qhd", score_grad, key_vecs, preferred_element_type=jnp.float32)
                * factor
            )
            key_total = (
                key_total
                + jnp.einsum(
                    "hqk,qhd->khd", score_grad, query_rows, preferred_element_type=jnp.float32
                )
                * factor
            )
            value_total = value_total + jnp.einsum(
                "hqk,qhd->khd",
                prob_rows.astype(jnp.bfloat16),
                grad_rows,
                preferred_element_type=jnp.float32,
            )
            return ((key_total, value_total), query_grad)

        start_totals = (
            jnp.zeros((SEQ, head_count, HD), jnp.float32),
            jnp.zeros((SEQ, head_count, HD), jnp.float32),
        )
        (key_total, value_total), query_grads = lax.scan(
            one_one_block, start_totals, jnp.arange(per_seq)
        )
        return (
            query_grads.reshape(SEQ, head_width),
            key_total.reshape(SEQ, head_width),
            value_total.reshape(SEQ, head_width),
        )

    query_grads, key_grads, value_grads = lax.map(one_sequence, jnp.arange(token_count // SEQ))
    stacked = jnp.stack(
        [
            query_grads.reshape(token_count, head_width),
            key_grads.reshape(token_count, head_width),
            value_grads.reshape(token_count, head_width),
        ],
        axis=1,
    )
    return stacked.astype(jnp.bfloat16)


def fold_rows(weight, saved_act, shard_piece):
    product = lax.dot_general(
        shard_piece, weight, (((1,), (1,)), ((), ())), preferred_element_type=jnp.float32
    )
    weight_total = lax.dot_general(
        saved_act, shard_piece, (((0,), (0,)), ((), ())), preferred_element_type=jnp.float32
    )
    return (product, weight_total)


def layer_forward(residual, weights, segments, tensor_rank):
    attn_w, out_w, up_w, down_w, gain_rows, bias_rows = weights
    gain_rows = gain_rows.astype(jnp.float32)
    bias_rows = bias_rows.astype(jnp.float32)
    local_rows = residual.shape[0]
    normed = layer_norm(residual, gain_rows[0], bias_rows[0]).astype(jnp.bfloat16)
    normed_full = lax.all_gather(normed, "tensor", axis=0, tiled=True)
    head_width = attn_w.shape[2]
    column = tensor_rank * head_width
    query_bias = lax.dynamic_slice_in_dim(bias_rows[1], column, head_width, 0)
    value_bias = lax.dynamic_slice_in_dim(bias_rows[2], column, head_width, 0)
    bias_three = jnp.stack([query_bias, jnp.zeros_like(query_bias), value_bias])
    project = (
        jnp.einsum("td,cde->tce", normed_full, attn_w, preferred_element_type=jnp.float32)
        + bias_three[None]
    ).astype(jnp.bfloat16)
    attended, log_total = attend(project, segments)

    def attn_term(first_row, row_count):
        return jnp.dot(attended, out_w, preferred_element_type=jnp.float32)

    middle = residual + (
        lax.psum_scatter(
            attn_term(jnp.int32(0), local_rows * lax.axis_size("tensor")),
            "tensor",
            scatter_dimension=0,
            tiled=True,
        )
        + bias_rows[3]
    )
    normed_two = layer_norm(middle, gain_rows[1], bias_rows[4]).astype(jnp.bfloat16)
    normed_two_kept = lax.all_gather(normed_two, "tensor", axis=0, tiled=True)
    unit_width = up_w.shape[1]
    up_bias = lax.dynamic_slice_in_dim(
        bias_rows[6:10].reshape(-1), tensor_rank * unit_width, unit_width, 0
    )
    hidden = jnp.dot(normed_two_kept, up_w, preferred_element_type=jnp.float32) + up_bias
    active = gelu_tanh(hidden).astype(jnp.bfloat16)
    output = middle + (
        lax.psum_scatter(
            jnp.dot(active, down_w, preferred_element_type=jnp.float32).astype(jnp.bfloat16),
            "tensor",
            scatter_dimension=0,
            tiled=True,
        ).astype(jnp.float32)
        + bias_rows[5]
    )
    return (
        output,
        (
            residual,
            middle,
            normed_full,
            project,
            attended,
            log_total,
            normed_two_kept,
            hidden,
            active,
        ),
    )


def layer_backward(upstream, weights, stored, segments, tensor_rank):
    attn_w, out_w, up_w, down_w, gain_rows, bias_rows = weights
    gain_rows = gain_rows.astype(jnp.float32)
    bias_rows = bias_rows.astype(jnp.float32)
    residual, middle, normed_full, project, attended, log_total, normed_two_kept, hidden, active = (
        stored
    )
    local_rows = upstream.shape[0]
    model_width = residual.shape[1]
    unit_width = up_w.shape[1]
    head_width = attn_w.shape[2]
    column = tensor_rank * head_width
    branch_grad = upstream.astype(jnp.bfloat16)
    down_bias_grad = jnp.sum(branch_grad.astype(jnp.float32), axis=0)
    active_grad, down_grad = fold_rows(
        down_w, active, lax.all_gather(branch_grad, "tensor", axis=0, tiled=True)
    )
    hidden_grad = jax.vjp(gelu_tanh, hidden)[1](active_grad)[0].astype(jnp.bfloat16)
    up_bias_grad = jnp.sum(hidden_grad.astype(jnp.float32), axis=0)
    up_rows_grad = lax.dynamic_update_slice_in_dim(
        jnp.zeros((4 * model_width,), jnp.float32), up_bias_grad, tensor_rank * unit_width, 0
    ).reshape(4, model_width)
    up_grad = lax.dot_general(
        normed_two_kept, hidden_grad, (((0,), (0,)), ((), ())), preferred_element_type=jnp.float32
    )
    normed_two_grad = lax.psum_scatter(
        lax.dot_general(
            hidden_grad, up_w, (((1,), (1,)), ((), ())), preferred_element_type=jnp.float32
        ),
        "tensor",
        scatter_dimension=0,
        tiled=True,
    )
    primal, pullback = jax.vjp(layer_norm, middle, gain_rows[1], bias_rows[4])
    middle_part, gain_two_grad, shift_two_grad = pullback(normed_two_grad)
    middle_grad = upstream + middle_part
    attn_branch = middle_grad.astype(jnp.bfloat16)
    out_bias_grad = jnp.sum(attn_branch.astype(jnp.float32), axis=0)
    attended_grad, out_grad = fold_rows(
        out_w, attended, lax.all_gather(attn_branch, "tensor", axis=0, tiled=True)
    )
    project_grad = attend_back(project, segments, log_total, attended_grad.astype(jnp.bfloat16))
    query_bias_grad = jnp.sum(project_grad[:, 0].astype(jnp.float32), axis=0)
    value_bias_grad = jnp.sum(project_grad[:, 2].astype(jnp.float32), axis=0)
    attn_grad = jnp.einsum(
        "td,tce->cde", normed_full, project_grad, preferred_element_type=jnp.float32
    )

    def attn_term(first_row, row_count):
        return jnp.einsum("tce,cde->td", project_grad, attn_w, preferred_element_type=jnp.float32)

    normed_grad = lax.psum_scatter(
        attn_term(jnp.int32(0), local_rows * lax.axis_size("tensor")).astype(jnp.bfloat16),
        "tensor",
        scatter_dimension=0,
        tiled=True,
    ).astype(jnp.float32)
    primal, pullback = jax.vjp(layer_norm, residual, gain_rows[0], bias_rows[0])
    residual_part, gain_one_grad, shift_one_grad = pullback(normed_grad)
    input_grad = middle_grad + residual_part
    query_full = lax.dynamic_update_slice_in_dim(
        jnp.zeros((model_width,), jnp.float32), query_bias_grad, column, 0
    )
    value_full = lax.dynamic_update_slice_in_dim(
        jnp.zeros((model_width,), jnp.float32), value_bias_grad, column, 0
    )
    gain_grad = jnp.stack([gain_one_grad, gain_two_grad])
    bias_grad = jnp.concatenate(
        [
            jnp.stack(
                [
                    shift_one_grad,
                    query_full,
                    value_full,
                    out_bias_grad,
                    shift_two_grad,
                    down_bias_grad,
                ]
            ),
            up_rows_grad,
        ],
        axis=0,
    )
    return (input_grad, (attn_grad, out_grad, up_grad, down_grad, gain_grad, bias_grad))


def per_device(
    activations,
    segments,
    attn_weight,
    out_weight,
    up_weight,
    down_weight,
    norm_gains,
    bias_rows,
    cotangent,
):
    tensor_rank = lax.axis_index("tensor")
    layers = attn_weight.shape[0]
    residual = activations.astype(jnp.float32)
    layer_index = 0
    weights = (
        lax.all_gather(attn_weight[layer_index], "dp", axis=1, tiled=True),
        lax.all_gather(out_weight[layer_index], "dp", axis=1, tiled=True),
        lax.all_gather(up_weight[layer_index], "dp", axis=0, tiled=True),
        lax.all_gather(down_weight[layer_index], "dp", axis=1, tiled=True),
        lax.all_gather(norm_gains[layer_index], "dp", axis=1, tiled=True),
        lax.all_gather(bias_rows[layer_index], "dp", axis=1, tiled=True),
    )
    residual, saved_now = layer_forward(residual, weights, segments, tensor_rank)
    stored = [saved_now]
    upstream = cotangent
    layer_grads = [None] * layers
    for layer_index in reversed(range(layers)):
        weights = (
            lax.all_gather(attn_weight[layer_index], "dp", axis=1, tiled=True),
            lax.all_gather(out_weight[layer_index], "dp", axis=1, tiled=True),
            lax.all_gather(up_weight[layer_index], "dp", axis=0, tiled=True),
            lax.all_gather(down_weight[layer_index], "dp", axis=1, tiled=True),
            lax.all_gather(norm_gains[layer_index], "dp", axis=1, tiled=True),
            lax.all_gather(bias_rows[layer_index], "dp", axis=1, tiled=True),
        )
        upstream, grads_now = layer_backward(
            upstream, weights, stored[layer_index], segments, tensor_rank
        )
        grads_now = (
            lax.psum_scatter(
                grads_now[0].astype(jnp.bfloat16), "dp", scatter_dimension=1, tiled=True
            ).astype(jnp.float32),
            lax.psum_scatter(
                grads_now[1].astype(jnp.bfloat16), "dp", scatter_dimension=1, tiled=True
            ).astype(jnp.float32),
            lax.psum_scatter(
                grads_now[2].astype(jnp.bfloat16), "dp", scatter_dimension=0, tiled=True
            ).astype(jnp.float32),
            lax.psum_scatter(
                grads_now[3].astype(jnp.bfloat16), "dp", scatter_dimension=1, tiled=True
            ).astype(jnp.float32),
            lax.psum_scatter(
                grads_now[4].astype(jnp.bfloat16), "dp", scatter_dimension=1, tiled=True
            ).astype(jnp.float32),
            lax.psum_scatter(
                grads_now[5].astype(jnp.bfloat16), "dp", scatter_dimension=1, tiled=True
            ).astype(jnp.float32),
        )
        layer_grads[layer_index] = grads_now
    stacked = tuple(
        (jnp.stack([layer_set[member] for layer_set in layer_grads]) for member in range(6))
    )
    small_sums = lax.psum((stacked[4], stacked[5]), "tensor")
    return (
        residual,
        upstream,
        stacked[0],
        stacked[1],
        stacked[2],
        stacked[3],
        small_sums[0],
        small_sums[1],
    )


def solution(mesh):
    return jax.shard_map(
        per_device,
        mesh=mesh,
        in_specs=(
            P(("dp", "tensor"), None),
            P("dp"),
            P(None, None, "dp", "tensor"),
            P(None, "tensor", "dp"),
            P(None, "dp", "tensor"),
            P(None, "tensor", "dp"),
            P(None, None, "dp"),
            P(None, None, "dp"),
            P(("dp", "tensor"), None),
        ),
        out_specs=(
            P(("dp", "tensor"), None),
            P(("dp", "tensor"), None),
            P(None, None, "dp", "tensor"),
            P(None, "tensor", "dp"),
            P(None, "dp", "tensor"),
            P(None, "tensor", "dp"),
            P(None, None, "dp"),
            P(None, None, "dp"),
        ),
        check_vma=False,
    )
```

profile of v0, /device:TPU:0, one launch (start us, length us, event | category | flops | bytes accessed | tf_op | source)
XLA Modules:
  0.0 839.7 jit_solution(1976598825178693592)
XLA Ops:
  7.9 10.3 %all-gather = bf16[1,2,1024]{2,1,0:T(2,128)(2,1)S(1)} all-gather(bf16[1,2,128]{2,1,0:T(2,128)(2,1)} %param.19), channel_id=2, replica_groups=mesh['dp'=8,'tensor'=4] {'dp'}, dimensions={2}, use_global_device_ids=true | all-gather | bytes 4608 | tf_op jit(solution)/shard_map/all_gather | solution.py:321
  18.3 8.7 %all-gather.1 = bf16[1,10,1024]{2,1,0:T(8,128)(2,1)S(1)} all-gather(bf16[1,10,128]{2,1,0:T(8,128)(2,1)} %param.20), channel_id=3, replica_groups=mesh['dp'=8,'tensor'=4] {'dp'}, dimensions={2}, use_global_device_ids=true | all-gather | bytes 23040 | tf_op jit(solution)/shard_map/all_gather | solution.py:322
  32.5 9.9 %all-gather.3 = bf16[1,256,1024]{2,1,0:T(8,128)(2,1)S(1)} all-gather(bf16[1,256,128]{2,1,0:T(8,128)(2,1)} %param.16), channel_id=5, replica_groups=mesh['dp'=8,'tensor'=4] {'dp'}, dimensions={2}, use_global_device_ids=true | all-gather | bytes 589824 | tf_op jit(solution)/shard_map/all_gather | solution.py:318
  42.4 44.5 %all-gather.14.cloned.1.call-done = bf16[1024,1024]{1,0:T(8,128)(2,1)} async-done(((bf16[256,1024]{1,0:T(8,128)(2,1)}), bf16[1024,1024]{1,0:T(8,128)(2,1)}) %all-gather.14.cloned.1.call-update) | async-done | bytes 2097168 | tf_op jit(solution)/shard_map/all_gather | solution.py:158
  93.6 18.3 %while.43 = (s32[]{:T(128)}, bf16[2,512,256]{2,1,0:T(8,128)(2,1)S(1)}, f32[2,4,512]{2,1,0:T(4,128)S(1)}, s32[2]{0:T(128)S(1)}, s32[1024]{0:T(1024)S(1)}, /*index...) while((s32[]{:T(128)}, ...), condition=%wide.region_5.6_spmd, body=%wide.region_2.5_spmd.sunk | while | flops 563740160 | bytes 32594288 | solution.py:68
  115.2 75.0 %reduce-scatter.21.cloned.1.call-done = f32[256,1024]{1,0:T(8,128)} async-done(((f32[1024,1024]{1,0:T(8,128)}), f32[256,1024]{1,0:T(8,128)}) %reduce-scatter.21.cloned.1.call-update) | async-done | bytes 1048592 | tf_op jit(solution)/shard_map/reduce_scatter | solution.py:174
  197.1 23.5 %all-gather.24.cloned.1.call-done = bf16[1,1024,1024]{2,1,0:T(8,128)(2,1)} async-done(((bf16[1,128,1024]{2,1,0:T(8,128)(2,1)}), bf16[1,1024,1024]{2,1,0:T(8,128)(2,1)}) %all-gather.24.cloned.1.call-update) | async-done | bytes 2097168 | tf_op jit(solution)/shard_map/all_gather | solution.py:319
  220.6 48.0 %all-gather.16.cloned.1.call-done = bf16[1024,1024]{1,0:T(8,128)(2,1)} async-done(((bf16[256,1024]{1,0:T(8,128)(2,1)}), bf16[1024,1024]{1,0:T(8,128)(2,1)}) %all-gather.16.cloned.1.call-update) | async-done | bytes 2097168 | tf_op jit(solution)/shard_map/all_gather | solution.py:183
  275.1 40.3 %all-gather.18.cloned.1.call-done = bf16[1024,1024]{1,0:T(8,128)(2,1)} async-done(((bf16[256,1024]{1,0:T(8,128)(2,1)}), bf16[1024,1024]{1,0:T(8,128)(2,1)}) %all-gather.18.cloned.1.call-update) | async-done | bytes 2097168 | tf_op jit(solution)/shard_map/all_gather | solution.py:230
  315.4 29.0 %all-gather.26.cloned.1.call-done = bf16[1,1024,1024]{2,1,0:T(8,128)(2,1)} async-done(((bf16[1,1024,128]{2,1,0:T(8,128)(2,1)}), bf16[1,1024,1024]{2,1,0:T(8,128)(2,1)}) %all-gather.26.cloned.1.call-update) | async-done | bytes 2097168 | tf_op jit(solution)/shard_map/all_gather | solution.py:320
  344.4 9.0 %convert_reduce_fusion = (bf16[1024]{0:T(1024)(128)(2,1)}, bf16[1024,1024]{1,0:T(8,128)(2,1)S(1)}) fusion(f32[1024,1024]{1,0:T(8,128)} %fusion.37, f32[1024]{0:T(1024)S(1)} %dynamic_slice.68, bf16[1024,1024]{1,0:T(8,128)(2,1)} %all-gather.18.cloned.1.call-done, bf16[1,1024,1024]{2,1,0:T(8,128)(2,1)} %all-gather.26.cloned.1.call-done), kind=kOutput, calls=%fused_computation.47 | convolution fusion | flops 2171599872 | bytes 10491904 | tf_op jit(solution)/shard_map/dot_general | solution.py:143
  359.1 7.0 fusion.43
  366.1 69.8 %reduce-scatter.25.cloned.1.call-done = f32[256,1024]{1,0:T(8,128)} async-done(((f32[1024,1024]{1,0:T(8,128)}), f32[256,1024]{1,0:T(8,128)}) %reduce-scatter.25.cloned.1.call-update) | async-done | bytes 1048592 | tf_op jit(solution)/shard_map/reduce_scatter | solution.py:240
  437.5 45.1 %reduce-scatter.23.cloned.1.call-done = bf16[256,1024]{1,0:T(8,128)(2,1)} async-done(((bf16[1024,1024]{1,0:T(8,128)(2,1)}), bf16[256,1024]{1,0:T(8,128)(2,1)}) %reduce-scatter.23.cloned.1.call-update) | async-done | bytes 524304 | tf_op jit(solution)/shard_map/reduce_scatter | solution.py:191
  486.8 7.2 convolution_convert_fusion
  504.2 27.8 %all-gather.20.cloned.1.call-done = bf16[1024,1024]{1,0:T(8,128)(2,1)} async-done(((bf16[256,1024]{1,0:T(8,128)(2,1)}), bf16[1024,1024]{1,0:T(8,128)(2,1)}) %all-gather.20.cloned.1.call-update) | async-done | bytes 2097168 | tf_op jit(solution)/shard_map/all_gather | solution.py:254
  540.5 34.0 %while.44 = (s32[]{:T(128)}, f32[1024,4,64]{0,2,1:T(8,128)S(1)}, f32[1024,4,64]{0,2,1:T(8,128)}, bf16[2,512,4,64]{1,3,2,0:T(8,128)(2,1)}, s32[2]{0:T(128)S(1)}, ...) while((s32[]{:T(128)}, f32[1024,4,64]{0,2,1:T(8,128)S(1)}, ...), condition=%wide.region_15.16_spmd.clone, body=%wide.region_13.15_spmd.clone.sunk | while | flops 1376648704 | bytes 88685112 | solution.py:121
  598.6 21.4 %reduce-scatter.29.cloned.1.call-done = bf16[128,1024]{1,0:T(8,128)(2,1)} async-done(((bf16[1024,1024]{1,0:T(8,128)(2,1)}), bf16[128,1024]{1,0:T(8,128)(2,1)}) %reduce-scatter.29.cloned.1.call-update) | async-done | bytes 262160 | tf_op jit(solution)/shard_map/reduce_scatter | solution.py:347
  623.2 34.3 %reduce-scatter.33.cloned.1.call-done = bf16[128,256]{1,0:T(8,128)(2,1)} async-done(((bf16[1024,256]{1,0:T(8,128)(2,1)}), bf16[128,256]{1,0:T(8,128)(2,1)}) %reduce-scatter.33.cloned.1.call-update) | async-done | bytes 65552
  659.2 40.0 %reduce-scatter.31.cloned.1.call-done = bf16[128,768]{1,0:T(8,128)(2,1)} async-done(((bf16[1024,768]{1,0:T(8,128)(2,1)}), bf16[128,768]{1,0:T(8,128)(2,1)}) %reduce-scatter.31.cloned.1.call-update) | async-done | bytes 196624
  701.4 43.8 %reduce-scatter.27.cloned.1.call-done = bf16[256,1024]{1,0:T(8,128)(2,1)} async-done(((bf16[1024,1024]{1,0:T(8,128)(2,1)}), bf16[256,1024]{1,0:T(8,128)(2,1)}) %reduce-scatter.27.cloned.1.call-update) | async-done | bytes 524304 | tf_op jit(solution)/shard_map/reduce_scatter | solution.py:266
  753.1 29.3 %reduce-scatter.37.cloned.1.call-done = bf16[128,2]{1,0:T(8,128)(2,1)} async-done(((bf16[1024,2]{1,0:T(8,128)(2,1)}), bf16[128,2]{1,0:T(8,128)(2,1)}) %reduce-scatter.37.cloned.1.call-update) | async-done | bytes 528
  783.2 35.7 %reduce-scatter.39.cloned.1.call-done = bf16[128,10]{1,0:T(8,128)(2,1)} async-done(((bf16[1024,10]{1,0:T(8,128)(2,1)}), bf16[128,10]{1,0:T(8,128)(2,1)}) %reduce-scatter.39.cloned.1.call-update) | async-done | bytes 2576
  819.7 12.6 %all-reduce = (f32[1,2,128]{2,1,0:T(2,128)}, f32[1,10,128]{2,1,0:T(8,128)S(1)}) all-reduce(f32[1,2,128]{2,1,0:T(2,128)S(1)} %bitcast_convert_fusion.6, f32[1,10,128]{2,1,0:T(8,128)S(1)} %bitcast_convert_fusion.5), channel_id=1, replica_groups=mesh['dp'=8,'tensor'=4] {'tensor'}, use_global_device_ids=true, to_apply=%region_26.27 | all-reduce | flops 1536 | bytes 12288 | tf_op jit(solution)/shard_map/psum | solution.py:364
  (252 shorter events, 145.7 us)
Async XLA Ops:
  7.2 35.3 %all-gather.22.cloned.1.call-start = ((), (), s32[]{:S(2)}) async-start(), calls=%async_computation.19 | async-start | bytes 1769472 | tf_op jit(solution)/shard_map/all_gather | solution.py:317
  7.9 79.0 %all-gather.14.cloned.1.call-start = ((), (), s32[]{:S(2)}) async-start(), calls=%async_computation.10 | async-start | bytes 2621440 | tf_op jit(solution)/shard_map/all_gather | solution.py:158
  32.3 157.9 %reduce-scatter.21.cloned.1.call-start = ((), (), s32[]{:S(2)}) async-start(), calls=%async_computation.11 | async-start | bytes 5242880 | tf_op jit(solution)/shard_map/reduce_scatter | solution.py:174
  114.6 106.0 %all-gather.24.cloned.1.call-start = ((), (), s32[]{:S(2)}) async-start(), calls=%async_computation.20 | async-start | bytes 2359296 | tf_op jit(solution)/shard_map/all_gather | solution.py:319
  115.2 153.4 %all-gather.16.cloned.1.call-start = ((), (), s32[]{:S(2)}) async-start(), calls=%async_computation.12 | async-start | bytes 2621440 | tf_op jit(solution)/shard_map/all_gather | solution.py:183
  193.0 122.3 %all-gather.18.cloned.1.call-start = ((), (), s32[]{:S(2)}) async-start(), calls=%async_computation.14 | async-start | bytes 2621440 | tf_op jit(solution)/shard_map/all_gather | solution.py:230
  195.8 148.6 %all-gather.26.cloned.1.call-start = ((), (), s32[]{:S(2)}) async-start(), calls=%async_computation.21 | async-start | bytes 2359296 | tf_op jit(solution)/shard_map/all_gather | solution.py:320
  196.5 239.4 %reduce-scatter.25.cloned.1.call-start = ((), (), s32[]{:S(2)}) async-start(), calls=%async_computation.15 | async-start | bytes 5242880 | tf_op jit(solution)/shard_map/reduce_scatter | solution.py:240
  359.0 123.6 %reduce-scatter.23.cloned.1.call-start = ((), (), s32[]{:S(2)}) async-start(), calls=%async_computation.13 | async-start | bytes 2621440 | tf_op jit(solution)/shard_map/reduce_scatter | solution.py:191
  366.1 165.9 %all-gather.20.cloned.1.call-start = ((), (), s32[]{:S(2)}) async-start(), calls=%async_computation.16 | async-start | bytes 2621440 | tf_op jit(solution)/shard_map/all_gather | solution.py:254
  486.6 110.0 %reduce-scatter.35.cloned.1.call-start = ((), (), s32[]{:S(2)}) async-start(), calls=%async_computation.24 | async-start | bytes 2359296
  498.1 121.9 %reduce-scatter.29.cloned.1.call-start = ((), (), s32[]{:S(2)}) async-start(), calls=%async_computation.18 | async-start | bytes 2359296 | tf_op jit(solution)/shard_map/reduce_scatter | solution.py:347
  504.1 153.4 %reduce-scatter.33.cloned.1.call-start = ((), (), s32[]{:S(2)}) async-start(), calls=%async_computation.23 | async-start | bytes 589824
  537.3 162.0 %reduce-scatter.31.cloned.1.call-start = ((), (), s32[]{:S(2)}) async-start(), calls=%async_computation.22 | async-start | bytes 1769472
  591.6 153.7 %reduce-scatter.27.cloned.1.call-start = ((), (), s32[]{:S(2)}) async-start(), calls=%async_computation.17 | async-start | bytes 2621440 | tf_op jit(solution)/shard_map/reduce_scatter | solution.py:266
  596.2 149.0 %copy-start.1 = (bf16[256,1024]{1,0:T(8,128)(2,1)S(1)}, bf16[256,1024]{1,0:T(8,128)(2,1)}, u32[]{:S(2)}) copy-start(bf16[256,1024]{1,0:T(8,128)(2,1)} %param.13) | copy-start | bytes 1572868
  596.2 149.0 %copy-start.18 = (f32[1,1,1024]{2,1,0:T(1,128)S(1)}, f32[1,1,1024]{2,1,0:T(1,128)}, u32[]{:S(2)}) copy-start(f32[1,1,1024]{2,1,0:T(1,128)} %copy-done.17) | copy-start | bytes 12292
  596.2 149.0 %copy-start.20 = (f32[256]{0:T(256)S(1)}, f32[256]{0:T(256)}, u32[]{:S(2)}) copy-start(f32[256]{0:T(256)} %copy-done.19) | copy-start | bytes 3076
  596.2 150.5 %copy-start.24 = (f32[256]{0:T(256)S(1)}, f32[256]{0:T(256)}, u32[]{:S(2)}) copy-start(f32[256]{0:T(256)} %copy-done.23) | copy-start | bytes 3076
  596.2 150.5 %copy-start.22 = (f32[256]{0:T(256)S(1)}, f32[256]{0:T(256)}, u32[]{:S(2)}) copy-start(f32[256]{0:T(256)} %copy-done.21) | copy-start | bytes 3076
  596.3 186.1 %reduce-scatter.37.cloned.1.call-start = ((), (), s32[]{:S(2)}) async-start(), calls=%async_computation.25 | async-start | bytes 294912
  598.6 153.0 %copy-start.3 = (f32[256,1024]{1,0:T(8,128)S(1)}, f32[256,1024]{1,0:T(8,128)}, u32[]{:S(2)}) copy-start(f32[256,1024]{1,0:T(8,128)} %param.21) | copy-start | bytes 3145732
  598.6 153.0 %copy-start.5 = (f32[256,1024]{1,0:T(8,128)S(1)}, f32[256,1024]{1,0:T(8,128)}, u32[]{:S(2)}) copy-start(f32[256,1024]{1,0:T(8,128)} %copy-done.4) | copy-start | bytes 3145732
  749.3 69.6 %reduce-scatter.39.cloned.1.call-start = ((), (), s32[]{:S(2)}) async-start(), calls=%async_computation.26 | async-start | bytes 294912
  (26 other events, 359.2 us)
Sparse Core Ops, SparseCore 0:
  9.9 28.6 all-gather.21
  40.7 46.1 all-gather.13
  114.7 75.4 reduce-scatter.20
  192.1 28.3 all-gather.23
  222.6 45.9 all-gather.15
  270.7 44.6 all-gather.17
  317.4 26.8 all-gather.25
  359.1 76.7 reduce-scatter.24
  438.2 44.3 reduce-scatter.22
  486.7 45.2 all-gather.19
  535.7 39.9 reduce-scatter.34
  578.8 41.2 reduce-scatter.28
  623.4 34.1 reduce-scatter.32
  660.7 38.4 reduce-scatter.30
  701.4 43.8 reduce-scatter.26
  749.5 32.8 reduce-scatter.36
  785.3 33.5 reduce-scatter.38
where the time goes:
time: 848 us; the launch traced here: 840 us
  waiting for transfers between devices  610 us (72%)
  matrix products  91.4 us (11%)
  blocking collectives  41.5 us (5%)
  other arithmetic  38.9 us (5%)
  local copies, waits for them, and re-layouts  35.2 us (4%)
  between operations  14.7 us (2%)
    unnamed x22, waiting for transfers between devices  141 us
    reduce_scatter x1, waiting for transfers between devices, layer_forward(): lax.psum_scatter(attn_term(jnp.int32(0), local_rows * lax.axis_size('tens...  75 us
    reduce_scatter x1, waiting for transfers between devices, layer_backward(): lax.psum_scatter(lax.dot_general(hidden_grad, up_w, (((1,), (1,)), ((), (...  69.8 us
    all_gather x1, waiting for transfers between devices, layer_forward(): normed_two_kept = lax.all_gather(normed_two, 'tensor', axis=0, tiled=True)  48 us
    reduce_scatter x1, waiting for transfers between devices, layer_forward(): lax.psum_scatter(jnp.dot(active, down_w, preferred_element_type=jnp.float...  45.1 us
    all_gather x1, waiting for transfers between devices, layer_forward(): normed_full = lax.all_gather(normed, 'tensor', axis=0, tiled=True)  44.5 us
    reduce_scatter x1, waiting for transfers between devices, layer_backward(): lax.psum_scatter(attn_term(jnp.int32(0), local_rows * lax.axis_size('tens...  43.8 us
    all_gather x1, waiting for transfers between devices, layer_backward(): lax.all_gather(branch_grad, 'tensor', axis=0, tiled=True)  40.3 us
  transfers between devices with their start and end apart: 17, of which 15 were waited for; matrix products, arithmetic and copies ran while one was open for 14% of the time, Pallas kernels for 0%

commit v1 on v0

v1 whole, which is shorter than its diff:
```python
import functools

import jax
import jax.numpy as jnp
from jax import lax
from jax.experimental import pallas as pl
from jax.experimental.pallas import tpu as pltpu
from jax.sharding import PartitionSpec as P

HD = 64
SEQ = 1024
EPSILON = 1e-05
MASKED = -1e30
MESH_ID = pl.DeviceIdType.MESH
BF = jnp.bfloat16
F32 = jnp.float32
ANY = pl.BlockSpec(memory_space=pl.ANY)
VM = pl.BlockSpec(memory_space=pltpu.VMEM)


def layer_norm(values, gain_row, shift_row):
    center = values - jnp.mean(values, axis=-1, keepdims=True)
    spread = jnp.mean(center * center, axis=-1, keepdims=True)
    return center * lax.rsqrt(spread + EPSILON) * gain_row + shift_row


def norm_stats(values):
    center = values - jnp.mean(values, axis=-1, keepdims=True)
    spread = jnp.mean(center * center, axis=-1, keepdims=True)
    scale = lax.rsqrt(spread + EPSILON)
    return center * scale, scale


def norm_back(grad, unit, scale, gain_row):
    u = grad * gain_row
    mean_u = jnp.mean(u, axis=-1, keepdims=True)
    mean_ux = jnp.mean(u * unit, axis=-1, keepdims=True)
    return scale * (u - mean_u - unit * mean_ux)


def gelu_tanh(values):
    return jax.nn.gelu(values, approximate=True)


class Geometry:
    def __init__(self, dp, tensor):
        self.dp, self.tensor = dp, tensor
        self.c_size = 2
        rest = dp // 2
        self.a_size = 1
        while self.a_size * self.a_size < rest:
            self.a_size *= 2
        self.b_size = rest // self.a_size
        assert self.a_size * self.b_size * 2 == dp

    def bind(self):
        spot = Spot()
        spot.geo = self
        spot.d = lax.axis_index("dp")
        spot.t = lax.axis_index("tensor")
        spot.c = lax.rem(spot.d, 2)
        half = lax.div(spot.d, 2)
        spot.a = lax.rem(half, self.a_size)
        spot.b = lax.div(half, self.a_size)
        return spot


class Spot:
    def rank(self, b, a, c):
        return (b * self.geo.a_size + a) * 2 + c

    def at_t(self, t):
        return (self.d, t)

    def at_d(self, d):
        return (d, self.t)


def ring_next(rank, step, size):
    return lax.rem(rank + step, size)


def ring_prev(rank, step, size):
    return lax.rem(rank + size - step, size)


class Wire:
    def __init__(self, send, recv):
        self.send_sems, self.recv_sems = send, recv
        self.count = 0
        self.pending = []

    def take(self, n):
        first = self.count
        self.count += n
        return first

    def copy(self, i, src, dst, device):
        return pltpu.make_async_remote_copy(
            src_ref=src, dst_ref=dst, send_sem=self.send_sems.at[i], recv_sem=self.recv_sems.at[i],
            device_id=device, device_id_type=MESH_ID)

    def start(self, i, src, dst, device, when=None):
        copy = self.copy(i, src, dst, device)
        if when is None:
            copy.start()
        else:
            pl.when(when)(copy.start)
        self.pending.append((copy, when))

    def landed(self, i, dst, device, when=None):
        copy = self.copy(i, dst, dst, device)
        if when is None:
            copy.wait_recv()
        else:
            pl.when(when)(copy.wait_recv)

    def drain(self):
        for copy, when in self.pending:
            if when is None:
                copy.wait_send()
            else:
                pl.when(when)(copy.wait_send)
        self.pending = []


def greet(spot, with_dp=True):
    geo = spot.geo
    barrier = pltpu.get_barrier_semaphore()
    total = 0
    for step in range(1, geo.tensor):
        pl.semaphore_signal(barrier, inc=1, device_id=spot.at_t(ring_next(spot.t, step, geo.tensor)), device_id_type=MESH_ID)
        total += 1
    for step in range(1, geo.dp):
        pl.semaphore_signal(barrier, inc=1, device_id=spot.at_d(ring_next(spot.d, step, geo.dp)), device_id_type=MESH_ID)
        total += 1
    pl.semaphore_wait(barrier, total)


class LineGather:
    def __init__(self, spot, wire, src, slot):
        self.spot, self.wire, self.src, self.slot = spot, wire, src, slot
        self.size = spot.geo.tensor
        self.line = self.size == 4
        self.first = wire.take(6 if self.line else self.size - 1)

    def start(self):
        spot, t = self.spot, self.spot.t
        if not self.line:
            for step in range(1, self.size):
                self.wire.start(self.first + step - 1, self.src, self.slot(t), spot.at_t(ring_next(t, step, self.size)))
            return
        for k, delta in enumerate((2, -2, 1, -1)):
            to = t + delta
            ok = (to >= 0) & (to < self.size)
            self.wire.start(self.first + k, self.src, self.slot(t), spot.at_t(to), when=ok)

    def forward(self):
        if not self.line:
            return
        spot, t = self.spot, self.spot.t
        self.wire.landed(self.first + 0, self.slot(t - 2), spot.at_t(t - 2), when=t == 2)
        self.wire.start(self.first + 4, self.slot(t - 2), self.slot(t - 2), spot.at_t(t + 1), when=t == 2)
        self.wire.landed(self.first + 1, self.slot(t + 2), spot.at_t(t + 2), when=t == 1)
        self.wire.start(self.first + 5, self.slot(t + 2), self.slot(t + 2), spot.at_t(t - 1), when=t == 1)

    def finish(self):
        spot, t = self.spot, self.spot.t
        if not self.line:
            for step in range(1, self.size):
                source = ring_prev(t, step, self.size)
                self.wire.landed(self.first + step - 1, self.slot(source), spot.at_t(source))
            return
        self.wire.landed(self.first + 0, self.slot(t - 2), spot.at_t(t - 2), when=t == 3)
        self.wire.landed(self.first + 1, self.slot(t + 2), spot.at_t(t + 2), when=t == 0)
        self.wire.landed(self.first + 2, self.slot(t - 1), spot.at_t(t - 1), when=t >= 1)
        self.wire.landed(self.first + 3, self.slot(t + 1), spot.at_t(t + 1), when=t <= 2)
        self.wire.landed(self.first + 4, self.slot(t - 3), spot.at_t(t - 1), when=t == 3)
        self.wire.landed(self.first + 5, self.slot(t + 3), spot.at_t(t + 1), when=t == 0)


class LineScatter:
    def __init__(self, spot, wire, part, land, add):
        self.spot, self.wire, self.part, self.land, self.add = spot, wire, part, land, add
        self.size = spot.geo.tensor
        self.line = self.size == 4
        self.first = wire.take(6 if self.line else self.size - 1)

    def start(self):
        spot, t = self.spot, self.spot.t
        if not self.line:
            for step in range(1, self.size):
                to = ring_next(t, step, self.size)
                self.wire.start(self.first + step - 1, self.part(to), self.land(step - 1), spot.at_t(to))
            return
        self.wire.start(self.first + 4, self.part(3), self.land(4), spot.at_t(1), when=t == 0)
        self.wire.start(self.first + 5, self.part(0), self.land(4), spot.at_t(2), when=t == 3)
        self.wire.start(self.first + 0, self.part(2), self.land(0), spot.at_t(2), when=t == 0)
        self.wire.start(self.first + 1, self.part(1), self.land(1), spot.at_t(1), when=t == 3)
        self.wire.start(self.first + 2, self.part(jnp.minimum(t + 1, 3)), self.land(2), spot.at_t(t + 1), when=t <= 2)
        self.wire.start(self.first + 3, self.part(jnp.maximum(t - 1, 0)), self.land(3), spot.at_t(t - 1), when=t >= 1)

    def forward(self):
        if not self.line:
            return
        spot, t = self.spot, self.spot.t

        @pl.when(t == 1)
        def _():
            self.wire.landed(self.first + 4, self.land(4), spot.at_t(0))
            self.add(self.part(3), self.land(4))

        @pl.when(t == 2)
        def _():
            self.wire.landed(self.first + 5, self.land(4), spot.at_t(3))
            self.add(self.part(0), self.land(4))

        self.wire.start(self.first + 0, self.part(3), self.land(0), spot.at_t(3), when=t == 1)
        self.wire.start(self.first + 1, self.part(0), self.land(1), spot.at_t(0), when=t == 2)

    def finish(self, total):
        spot, t = self.spot, self.spot.t
        if not self.line:
            for step in range(1, self.size):
                self.wire.landed(self.first + step - 1, self.land(step - 1), spot.at_t(ring_prev(t, step, self.size)))
                total(self.land(step - 1))
            return
        for k, delta in enumerate((2, -2, 1, -1)):
            source = t - delta

            @pl.when((source >= 0) & (source < self.size))
            def _():
                self.wire.landed(self.first + k, self.land(k), spot.at_t(source))
                total(self.land(k))


def add_into(rows):
    def add(dst, src):
        dst[...] = (dst[...].astype(F32) + src[...].astype(F32)).astype(dst.dtype)

    return add


def add_tiled(dst, src, tile):
    count = dst.shape[0] // tile

    def step(i, carry):
        rows = pl.ds(pl.multiple_of(i * tile, tile), tile)
        dst[rows] = (dst[rows].astype(F32) + src[rows].astype(F32)).astype(dst.dtype)
        return carry

    lax.fori_loop(0, count, step, 0)


def k1_body(geo, x_ref, w_ref, s_ref, xf, wf, sf, send, recv, local):
    spot = geo.bind()
    wire = Wire(send, recv)
    rows = x_ref.shape[0]
    wrows = w_ref.shape[1]

    def slot(t):
        return xf.at[pl.ds(pl.multiple_of(t * rows, rows), rows)]

    def wslot(d):
        return wf.at[:, pl.ds(pl.multiple_of(d * wrows, wrows), wrows)]

    own = [
        pltpu.make_async_copy(x_ref, slot(spot.t), local.at[0]),
        pltpu.make_async_copy(w_ref, wslot(spot.d), local.at[1]),
        pltpu.make_async_copy(s_ref, sf.at[spot.d], local.at[2]),
    ]
    for copy in own:
        copy.start()
    greet(spot)
    gather = LineGather(spot, wire, x_ref, slot)
    gather.start()
    small = wire.take(geo.dp - 1)
    big = wire.take(geo.dp - 1)
    for step in range(1, geo.dp):
        to = ring_next(spot.d, step, geo.dp)
        wire.start(small + step - 1, s_ref, sf.at[spot.d], spot.at_d(to))
        wire.start(big + step - 1, w_ref, wslot(spot.d), spot.at_d(to))
    gather.forward()
    for step in range(1, geo.dp):
        source = ring_prev(spot.d, step, geo.dp)
        wire.landed(small + step - 1, sf.at[source], spot.at_d(source))
        wire.landed(big + step - 1, wslot(source), spot.at_d(source))
    gather.finish()
    wire.drain()
    for copy in own:
        copy.wait()


def k1(geo, x, w4, small):
    sems = 6 + 2 * geo.dp + geo.tensor
    return pl.pallas_call(
        functools.partial(k1_body, geo),
        out_shape=(
            jax.ShapeDtypeStruct((geo.tensor * x.shape[0], x.shape[1]), BF),
            jax.ShapeDtypeStruct((w4.shape[0], geo.dp * w4.shape[1], w4.shape[2]), BF),
            jax.ShapeDtypeStruct((geo.dp,) + small.shape, small.dtype),
        ),
        in_specs=[ANY] * 3,
        out_specs=(ANY, ANY, ANY),
        scratch_shapes=[pltpu.SemaphoreType.DMA((sems,)), pltpu.SemaphoreType.DMA((sems,)), pltpu.SemaphoreType.DMA((3,))],
        compiler_params=pltpu.CompilerParams(collective_id=1, has_side_effects=True),
        name="k1",
    )(x, w4, small)


class WeightGather:
    def __init__(self, spot, wire, piece, full):
        geo = spot.geo
        self.spot, self.wire, self.piece, self.full = spot, wire, piece, full
        self.rows = piece.shape[0]
        self.line = LineGather(spot, wire, piece, lambda t: full.at[t, self.span(spot.d)])
        self.one_a = wire.take(geo.a_size - 1)
        self.one_b = wire.take(geo.b_size - 1)
        self.two_a = wire.take((geo.b_size - 1) * geo.a_size)
        self.two_b = wire.take((geo.a_size - 1) * geo.b_size)
        self.last = wire.take(geo.a_size * geo.b_size)
        self.half = geo.tensor // 2

    def span(self, d):
        return pl.ds(pl.multiple_of(d * self.rows, self.rows), self.rows)

    def low(self, d):
        return self.full.at[pl.ds(0, self.half), self.span(d)]

    def high(self, d):
        return self.full.at[pl.ds(self.half, self.spot.geo.tensor - self.half), self.span(d)]

    def both(self, d):
        return self.full.at[:, self.span(d)]

    def first(self):
        spot, geo = self.spot, self.spot.geo
        mine = spot.d
        for j in range(1, geo.a_size):
            to = spot.rank(spot.b, ring_next(spot.a, j, geo.a_size), spot.c)
            self.wire.start(self.one_a + j - 1, self.low(mine), self.low(mine), spot.at_d(to))
        for j in range(1, geo.b_size):
            to = spot.rank(ring_next(spot.b, j, geo.b_size), spot.a, spot.c)
            self.wire.start(self.one_b + j - 1, self.high(mine), self.high(mine), spot.at_d(to))
        sibling = spot.rank(spot.b, spot.a, 1 - spot.c)
        self.wire.start(self.last, self.both(mine), self.both(mine), spot.at_d(sibling))

    def second(self):
        spot, geo = self.spot, self.spot.geo
        for i in range(geo.a_size):
            held = spot.rank(spot.b, ring_prev(spot.a, i, geo.a_size), spot.c)
            if i:
                self.wire.landed(self.one_a + i - 1, self.low(held), spot.at_d(held))
            for j in range(1, geo.b_size):
                to = spot.rank(ring_next(spot.b, j, geo.b_size), spot.a, spot.c)
                self.wire.start(self.two_a + (j - 1) * geo.a_size + i, self.low(held), self.low(held), spot.at_d(to))
        for i in range(geo.b_size):
            held = spot.rank(ring_prev(spot.b, i, geo.b_size), spot.a, spot.c)
            if i:
                self.wire.landed(self.one_b + i - 1, self.high(held), spot.at_d(held))
            for j in range(1, geo.a_size):
                to = spot.rank(spot.b, ring_next(spot.a, j, geo.a_size), spot.c)
                self.wire.start(self.two_b + (j - 1) * geo.b_size + i, self.high(held), self.high(held), spot.at_d(to))

    def third(self):
        spot, geo = self.spot, self.spot.geo
        for j in range(1, geo.b_size):
            for i in range(geo.a_size):
                held = spot.rank(ring_prev(spot.b, j, geo.b_size), ring_prev(spot.a, i, geo.a_size), spot.c)
                source = spot.rank(ring_prev(spot.b, j, geo.b_size), spot.a, spot.c)
                self.wire.landed(self.two_a + (j - 1) * geo.a_size + i, self.low(held), spot.at_d(source))
        for j in range(1, geo.a_size):
            for i in range(geo.b_size):
                held = spot.rank(ring_prev(spot.b, i, geo.b_size), ring_prev(spot.a, j, geo.a_size), spot.c)
                source = spot.rank(spot.b, ring_prev(spot.a, j, geo.a_size), spot.c)
                self.wire.landed(self.two_b + (j - 1) * geo.b_size + i, self.high(held), spot.at_d(source))
        sibling = spot.rank(spot.b, spot.a, 1 - spot.c)
        for j in range(geo.b_size):
            for i in range(geo.a_size):
                if i or j:
                    held = spot.rank(ring_prev(spot.b, j, geo.b_size), ring_prev(spot.a, i, geo.a_size), spot.c)
                    self.wire.start(self.last + j * geo.a_size + i, self.both(held), self.both(held), spot.at_d(sibling))

    def fourth(self):
        spot, geo = self.spot, self.spot.geo
        sibling = spot.rank(spot.b, spot.a, 1 - spot.c)
        for j in range(geo.b_size):
            for i in range(geo.a_size):
                held = spot.rank(ring_prev(spot.b, j, geo.b_size), ring_prev(spot.a, i, geo.a_size), 1 - spot.c)
                self.wire.landed(self.last + j * geo.a_size + i, self.both(held), spot.at_d(sibling))


def gather_sems(geo):
    ab = geo.a_size * geo.b_size
    return 6 + geo.tensor + geo.a_size + geo.b_size + 3 * ab


def k2_body(geo, part, m_ref, total, full, land, send, recv, local):
    spot = geo.bind()
    wire = Wire(send, recv)
    rows = total.shape[0]
    mrows = m_ref.shape[1]

    def block(t):
        return part.at[pl.ds(pl.multiple_of(t * rows, rows), rows)]

    own = []
    for k in range(2):
        span = pl.ds(pl.multiple_of(spot.d * mrows, mrows), mrows)
        copy = pltpu.make_async_copy(m_ref.at[k], full.at[k, spot.t, span], local.at[k])
        copy.start()
        own.append(copy)
    greet(spot)
    scatter = LineScatter(spot, wire, block, lambda k: land.at[k], lambda dst, src: add_tiled(dst, src, 64))
    gathers = [WeightGather(spot, wire, m_ref.at[k], full.at[k]) for k in range(2)]
    gathers[0].line.start()
    scatter.start()
    gathers[1].line.start()
    gathers[0].line.forward()
    scatter.forward()
    own[0].wait()
    gathers[0].line.finish()
    gathers[0].first()
    gathers[1].line.forward()
    own[1].wait()
    gathers[1].line.finish()
    gathers[1].first()
    gathers[0].second()
    gathers[1].second()

    mine = block(spot.t)

    def set_total(i, carry):
        span = pl.ds(pl.multiple_of(i * 64, 64), 64)
        total[span] = mine[span].astype(F32)
        return carry

    lax.fori_loop(0, rows // 64, set_total, 0)
    scatter.finish(lambda ref: add_tiled(total, ref, 64))
    gathers[0].third()
    gathers[1].third()
    gathers[0].fourth()
    gathers[1].fourth()
    wire.drain()


def k2(geo, part, m2):
    sems = 6 + geo.tensor + 2 * gather_sems(geo)
    rows = part.shape[0] // geo.tensor
    width = part.shape[1]
    return pl.pallas_call(
        functools.partial(k2_body, geo),
        out_shape=(
            jax.ShapeDtypeStruct((rows, width), F32),
            jax.ShapeDtypeStruct((2, geo.tensor, geo.dp * m2.shape[1], m2.shape[2]), BF),
        ),
        in_specs=[VM, ANY],
        out_specs=(VM, ANY),
        scratch_shapes=[
            pltpu.VMEM((max(5, geo.tensor - 1), rows, width), BF),
            pltpu.SemaphoreType.DMA((sems,)), pltpu.SemaphoreType.DMA((sems,)), pltpu.SemaphoreType.DMA((2,))],
        compiler_params=pltpu.CompilerParams(collective_id=2, has_side_effects=True, vmem_limit_bytes=32 * 2**20),
        name="k2",
    )(part, m2)


class WeightScatter:
    def __init__(self, spot, wire, part, held, mine, one_a, one_b, two_a, two_b, land, sem):
        geo = spot.geo
        self.spot, self.wire, self.part, self.held, self.mine = spot, wire, part, held, mine
        self.one_a_buf, self.one_b_buf, self.two_a_buf, self.two_b_buf = one_a, one_b, two_a, two_b
        self.sem = sem
        self.rows = held.shape[3]
        self.half = geo.tensor // 2
        ab = geo.a_size * geo.b_size
        self.zero = wire.take(ab)
        self.one_a = wire.take(geo.a_size - 1)
        self.one_b = wire.take(geo.b_size - 1)
        self.two_a = wire.take(geo.b_size - 1)
        self.two_b = wire.take(geo.a_size - 1)
        here = held.at[spot.b, spot.a]
        self.line = LineScatter(spot, wire, lambda t: here.at[t], lambda k: land.at[k], lambda dst, src: add_tiled(dst, src, min(64, self.rows)))

    def span(self, d):
        return pl.ds(pl.multiple_of(d * self.rows, self.rows), self.rows)

    def start(self):
        spot, geo = self.spot, self.spot.geo
        sibling = spot.rank(spot.b, spot.a, 1 - spot.c)
        self.loads = []
        for b in range(geo.b_size):
            for a in range(geo.a_size):
                theirs = self.part.at[:, self.span(spot.rank(b, a, 1 - spot.c))]
                self.wire.start(self.zero + b * geo.a_size + a, theirs, self.held.at[b, a], spot.at_d(sibling))
                ours = self.part.at[:, self.span(spot.rank(b, a, spot.c))]
                load = pltpu.make_async_copy(ours, self.mine.at[b, a], self.sem.at[b * geo.a_size + a])
                load.start()
                self.loads.append(load)

    def add(self, dst, src):
        n = dst.shape[0]
        tile = min(64, self.rows)
        per = self.rows // tile

        def step(i, carry):
            rows = pl.ds(pl.multiple_of(lax.rem(i, per) * tile, tile), tile)
            j = lax.div(i, per)
            dst[j, rows] = (dst[j, rows].astype(F32) + src[j, rows].astype(F32)).astype(dst.dtype)
            return carry

        lax.fori_loop(0, n * per, step, 0)

    def first(self):
        spot, geo = self.spot, self.spot.geo
        sibling = spot.rank(spot.b, spot.a, 1 - spot.c)
        for b in range(geo.b_size):
            for a in range(geo.a_size):
                i = b * geo.a_size + a
                self.loads[i].wait()
                self.wire.landed(self.zero + i, self.held.at[b, a], spot.at_d(sibling))
                self.add(self.held.at[b, a], self.mine.at[b, a])
        for j in range(1, geo.a_size):
            a = ring_next(spot.a, j, geo.a_size)
            to = spot.rank(spot.b, a, spot.c)
            self.wire.start(self.one_a + j - 1, self.held.at[:, a, pl.ds(0, self.half)], self.one_a_buf.at[j - 1], spot.at_d(to))
        for j in range(1, geo.b_size):
            b = ring_next(spot.b, j, geo.b_size)
            to = spot.rank(b, spot.a, spot.c)
            self.wire.start(self.one_b + j - 1, self.held.at[b, :, pl.ds(self.half, self.half)], self.one_b_buf.at[j - 1], spot.at_d(to))

    def second(self):
        spot, geo = self.spot, self.spot.geo
        low, high = pl.ds(0, self.half), pl.ds(self.half, self.half)
        for j in range(1, geo.a_size):
            self.wire.landed(self.one_a + j - 1, self.one_a_buf.at[j - 1], spot.at_d(spot.rank(spot.b, ring_prev(spot.a, j, geo.a_size), spot.c)))
            for b in range(geo.b_size):
                self.add(self.held.at[b, spot.a, low], self.one_a_buf.at[j - 1, b])
        for j in range(1, geo.b_size):
            b = ring_next(spot.b, j, geo.b_size)
            self.wire.start(self.two_a + j - 1, self.held.at[b, spot.a, low], self.two_a_buf.at[j - 1], spot.at_d(spot.rank(b, spot.a, spot.c)))
        for j in range(1, geo.b_size):
            self.wire.landed(self.one_b + j - 1, self.one_b_buf.at[j - 1], spot.at_d(spot.rank(ring_prev(spot.b, j, geo.b_size), spot.a, spot.c)))
            for a in range(geo.a_size):
                self.add(self.held.at[spot.b, a, high], self.one_b_buf.at[j - 1, a])
        for j in range(1, geo.a_size):
            a = ring_next(spot.a, j, geo.a_size)
            self.wire.start(self.two_b + j - 1, self.held.at[spot.b, a, high], self.two_b_buf.at[j - 1], spot.at_d(spot.rank(spot.b, a, spot.c)))

    def third(self):
        spot, geo = self.spot, self.spot.geo
        low, high = pl.ds(0, self.half), pl.ds(self.half, self.half)
        for j in range(1, geo.b_size):
            self.wire.landed(self.two_a + j - 1, self.two_a_buf.at[j - 1], spot.at_d(spot.rank(ring_prev(spot.b, j, geo.b_size), spot.a, spot.c)))
            self.add(self.held.at[spot.b, spot.a, low], self.two_a_buf.at[j - 1])
        for j in range(1, geo.a_size):
            self.wire.landed(self.two_b + j - 1, self.two_b_buf.at[j - 1], spot.at_d(spot.rank(spot.b, ring_prev(spot.a, j, geo.a_size), spot.c)))
            self.add(self.held.at[spot.b, spot.a, high], self.two_b_buf.at[j - 1])
        self.line.start()

    def fourth(self, out):
        spot = self.spot
        self.line.forward()
        here = self.held.at[spot.b, spot.a, spot.t]
        tile = min(64, self.rows)

        def step(i, carry):
            rows = pl.ds(pl.multiple_of(i * tile, tile), tile)
            out[rows] = here[rows].astype(F32)
            return carry

        lax.fori_loop(0, self.rows // tile, step, 0)
        self.line.finish(lambda ref: add_tiled(out, ref, tile))


def k3_body(geo, ga_ref, g_ref, gaf, out, *rest):
    *bufs, send, recv, local, loads = rest
    spot = geo.bind()
    wire = Wire(send, recv)
    rows = ga_ref.shape[0]

    def slot(t):
        return gaf.at[pl.ds(pl.multiple_of(t * rows, rows), rows)]

    own = pltpu.make_async_copy(ga_ref, slot(spot.t), local.at[0])
    own.start()
    greet(spot)
    gather = LineGather(spot, wire, ga_ref, slot)
    scatters = [WeightScatter(spot, wire, g_ref.at[k], *(buf.at[k] for buf in bufs), loads.at[k]) for k in range(2)]
    scatters[1].start()
    scatters[0].start()
    gather.start()
    scatters[1].first()
    scatters[0].first()
    gather.forward()
    scatters[1].second()
    scatters[0].second()
    scatters[1].third()
    scatters[0].third()
    gather.finish()
    scatters[1].fourth(out.at[1])
    scatters[0].fourth(out.at[0])
    wire.drain()
    own.wait()


def k3(geo, ga, grads):
    rows = grads.shape[2] // geo.dp
    width = grads.shape[3]
    t, a, b = geo.tensor, geo.a_size, geo.b_size
    ab = a * b
    half = t // 2
    sems = 12 + 2 * t + 2 * (ab + 2 * a + 2 * b + 6)
    return pl.pallas_call(
        functools.partial(k3_body, geo),
        out_shape=(
            jax.ShapeDtypeStruct((t * ga.shape[0], ga.shape[1]), BF),
            jax.ShapeDtypeStruct((2, rows, width), F32),
        ),
        in_specs=[ANY, ANY],
        out_specs=(ANY, VM),
        scratch_shapes=[
            pltpu.VMEM((2, b, a, t, rows, width), BF),
            pltpu.VMEM((2, b, a, t, rows, width), BF),
            pltpu.VMEM((2, a - 1, b, half, rows, width), BF),
            pltpu.VMEM((2, b - 1, a, half, rows, width), BF),
            pltpu.VMEM((2, b - 1, half, rows, width), BF),
            pltpu.VMEM((2, a - 1, half, rows, width), BF),
            pltpu.VMEM((2, max(5, t - 1), rows, width), BF),
            pltpu.SemaphoreType.DMA((sems,)), pltpu.SemaphoreType.DMA((sems,)),
            pltpu.SemaphoreType.DMA((1,)), pltpu.SemaphoreType.DMA((2, ab))],
        compiler_params=pltpu.CompilerParams(collective_id=3, has_side_effects=True, vmem_limit_bytes=56 * 2**20),
        name="k3",
    )(ga, grads)


def k4_body(geo, part, w_ref, s_ref, total, wout, sout, land, wland, sland, stot, tland, send, recv):
    spot = geo.bind()
    wire = Wire(send, recv)
    rows = total.shape[0]
    wrows = wout.shape[1]
    greet(spot)

    def block(t):
        return part.at[pl.ds(pl.multiple_of(t * rows, rows), rows)]

    def wblock(d):
        return w_ref.at[:, pl.ds(pl.multiple_of(d * wrows, wrows), wrows)]

    small = wire.take(geo.dp - 1)
    big = wire.take(geo.dp - 1)
    last = wire.take(geo.tensor - 1)
    scatter = LineScatter(spot, wire, block, lambda k: land.at[k], lambda dst, src: add_tiled(dst, src, 64))
    scatter.start()
    for step in range(1, geo.dp):
        to = ring_next(spot.d, step, geo.dp)
        wire.start(small + step - 1, s_ref.at[to], sland.at[step - 1], spot.at_d(to))
    for step in range(1, geo.dp):
        to = ring_next(spot.d, step, geo.dp)
        wire.start(big + step - 1, wblock(to), wland.at[step - 1], spot.at_d(to))
    stot[...] = s_ref[spot.d]
    for step in range(1, geo.dp):
        wire.landed(small + step - 1, sland.at[step - 1], spot.at_d(ring_prev(spot.d, step, geo.dp)))
        stot[...] += sland[step - 1]
    for step in range(1, geo.tensor):
        wire.start(last + step - 1, stot, tland.at[step - 1], spot.at_t(ring_next(spot.t, step, geo.tensor)))
    scatter.forward()
    own = wblock(spot.d)
    for k in range(w_ref.shape[0]):
        wout[k] = own[k].astype(F32)
    for step in range(1, geo.dp):
        wire.landed(big + step - 1, wland.at[step - 1], spot.at_d(ring_prev(spot.d, step, geo.dp)))

        def add(k, carry):
            wout[k] += wland[step - 1, k].astype(F32)
            return carry

        lax.fori_loop(0, w_ref.shape[0], add, 0)
    sout[...] = stot[...]
    for step in range(1, geo.tensor):
        wire.landed(last + step - 1, tland.at[step - 1], spot.at_t(ring_prev(spot.t, step, geo.tensor)))
        sout[...] += tland[step - 1]
    mine = block(spot.t)

    def set_total(i, carry):
        span = pl.ds(pl.multiple_of(i * 64, 64), 64)
        total[span] = mine[span].astype(F32)
        return carry

    lax.fori_loop(0, rows // 64, set_total, 0)
    scatter.finish(lambda ref: add_tiled(total, ref, 64))
    wire.drain()


def k4(geo, part, wgrad, small):
    rows = part.shape[0] // geo.tensor
    width = part.shape[1]
    wshape = (wgrad.shape[0], wgrad.shape[1] // geo.dp, wgrad.shape[2])
    sshape = small.shape[1:]
    sems = 6 + 2 * geo.tensor + 2 * geo.dp
    return pl.pallas_call(
        functools.partial(k4_body, geo),
        out_shape=(
            jax.ShapeDtypeStruct((rows, width), F32),
            jax.ShapeDtypeStruct(wshape, F32),
            jax.ShapeDtypeStruct(sshape, F32),
        ),
        in_specs=[VM, VM, VM],
        out_specs=(VM, VM, VM),
        scratch_shapes=[
            pltpu.VMEM((max(5, geo.tensor - 1), rows, width), BF),
            pltpu.VMEM((geo.dp - 1,) + wshape, BF),
            pltpu.VMEM((geo.dp - 1,) + sshape, F32),
            pltpu.VMEM(sshape, F32),
            pltpu.VMEM((geo.tensor - 1,) + sshape, F32),
            pltpu.SemaphoreType.DMA((sems,)), pltpu.SemaphoreType.DMA((sems,))],
        compiler_params=pltpu.CompilerParams(collective_id=4, has_side_effects=True, vmem_limit_bytes=48 * 2**20),
        name="k4",
    )(part, wgrad, small)


def visible_mask(segments, first_row, block_rows):
    query_pos = first_row + jnp.arange(block_rows)
    key_pos = jnp.arange(SEQ)
    query_seg = lax.dynamic_slice_in_dim(segments, first_row, block_rows, 0)
    return (key_pos[None, :] <= query_pos[:, None]) & (query_seg[:, None] == segments[None, :])


def block_scores(project, segments, first_row, block_rows):
    head_count = project.shape[2] // HD
    query_rows = lax.dynamic_slice_in_dim(project, first_row, block_rows, 1)[0].reshape(block_rows, head_count, HD)
    key_vecs = project[1].reshape(SEQ, head_count, HD)
    value_vecs = project[2].reshape(SEQ, head_count, HD)
    scores = jnp.einsum("qhd,khd->hqk", query_rows, key_vecs, preferred_element_type=F32) * HD ** (-0.5)
    visible = visible_mask(segments, first_row, block_rows)
    scores = jnp.where(visible[None], scores, MASKED)
    return (query_rows, key_vecs, value_vecs, scores)


def attend(project, segments):
    block_rows = 512

    def one(block_index):
        first_row = block_index * block_rows
        query_rows, key_vecs, value_vecs, scores = block_scores(project, segments, first_row, block_rows)
        row_max = jnp.max(scores, axis=-1, keepdims=True)
        raised = jnp.exp(scores - row_max)
        row_total = jnp.sum(raised, axis=-1, keepdims=True)
        prob_rows = (raised / row_total).astype(BF)
        attended = jnp.einsum("hqk,khd->qhd", prob_rows, value_vecs, preferred_element_type=F32)
        return attended.reshape(block_rows, -1).astype(BF), (row_max + jnp.log(row_total))[:, :, 0]

    attended, log_total = lax.map(one, jnp.arange(SEQ // block_rows))
    return (attended.reshape(SEQ, -1), log_total)


def attend_back(project, segments, log_total, attended_grad):
    head_width = project.shape[2]
    head_count = head_width // HD
    block_rows = 512
    factor = HD ** (-0.5)

    def one(totals, index):
        key_total, value_total = totals
        first_row = index * block_rows
        query_rows, key_vecs, value_vecs, scores = block_scores(project, segments, first_row, block_rows)
        prob_rows = jnp.exp(scores - log_total[index][:, :, None])
        grad_rows = lax.dynamic_slice_in_dim(attended_grad, first_row, block_rows, 0).reshape(block_rows, head_count, HD)
        prob_grad = jnp.einsum("qhd,khd->hqk", grad_rows, value_vecs, preferred_element_type=F32)
        inner_sum = jnp.sum(prob_rows * prob_grad, axis=-1, keepdims=True)
        score_grad = (prob_rows * (prob_grad - inner_sum)).astype(BF)
        query_grad = jnp.einsum("hqk,khd->qhd", score_grad, key_vecs, preferred_element_type=F32) * factor
        key_total = key_total + jnp.einsum("hqk,qhd->khd", score_grad, query_rows, preferred_element_type=F32) * factor
        value_total = value_total + jnp.einsum("hqk,qhd->khd", prob_rows.astype(BF), grad_rows, preferred_element_type=F32)
        return ((key_total, value_total), query_grad)

    zero = jnp.zeros((SEQ, head_count, HD), F32)
    (key_total, value_total), query_grads = lax.scan(one, (zero, zero), jnp.arange(SEQ // block_rows))
    stacked = jnp.stack([query_grads.reshape(SEQ, head_width), key_total.reshape(SEQ, head_width), value_total.reshape(SEQ, head_width)])
    return stacked.astype(BF)


def dot_nt(x, w):
    return lax.dot_general(x, w, (((1,), (1,)), ((), ())), preferred_element_type=F32)


def dot_tn(x, w):
    return lax.dot_general(x, w, (((0,), (0,)), ((), ())), preferred_element_type=F32)


def per_device(geo, activations, segments, attn_weight, out_weight, up_weight, down_weight, norm_gains, bias_rows, cotangent):
    tensor_rank = lax.axis_index("tensor")
    width = activations.shape[1]
    head_width = attn_weight.shape[3]
    w4 = jnp.concatenate([attn_weight[0], out_weight.transpose(0, 2, 1)], axis=0)
    m2 = jnp.concatenate([up_weight, down_weight.transpose(0, 2, 1)], axis=0)
    small = jnp.concatenate([norm_gains[0], bias_rows[0]], axis=0)
    x_full, w_full, small_full = k1(geo, activations, w4, small)
    rows12 = small_full.transpose(1, 0, 2).reshape(12, width).astype(F32)
    gains, biases = rows12[:2], rows12[2:]
    column = tensor_rank * head_width

    normed_full = layer_norm(x_full.astype(F32), gains[0], biases[0]).astype(BF)
    query_bias = lax.dynamic_slice_in_dim(biases[1], column, head_width, 0)
    value_bias = lax.dynamic_slice_in_dim(biases[2], column, head_width, 0)
    bias_three = jnp.stack([query_bias, jnp.zeros_like(query_bias), value_bias])
    project = (jnp.einsum("td,cde->cte", normed_full, w_full[:3], preferred_element_type=F32) + bias_three[:, None]).astype(BF)
    attended, log_total = attend(project, segments)
    attn_part = dot_nt(attended, w_full[3]).astype(BF)
    attn_sum, m_full = k2(geo, attn_part, m2)

    residual = activations.astype(F32)
    middle = residual + (attn_sum + biases[3])
    unit_two, scale_two = norm_stats(middle)
    normed_two = (unit_two * gains[1] + biases[4]).astype(BF)
    up_full, down_full = m_full[0], m_full[1]
    tensor = up_full.shape[0]
    unit_width = up_full.shape[2]
    up_bias = biases[6:10].reshape(1, -1)
    hidden = jnp.concatenate([jnp.dot(normed_two, up_full[s], preferred_element_type=F32) for s in range(tensor)], axis=1) + up_bias
    active = gelu_tanh(hidden).astype(BF)
    branch = cotangent.astype(BF)
    ff = sum(dot_nt(active[:, s * unit_width:(s + 1) * unit_width], down_full[s]) for s in range(tensor))
    output = middle + (ff + biases[5])
    active_grad = jnp.concatenate([jnp.dot(branch, down_full[s], preferred_element_type=F32) for s in range(tensor)], axis=1)
    hidden_grad = jax.vjp(gelu_tanh, hidden)[1](active_grad)[0].astype(BF)
    up_bias_grad = jnp.sum(hidden_grad.astype(F32), axis=0).reshape(4, width)
    grads = jnp.stack([
        jnp.stack([dot_tn(normed_two, hidden_grad[:, s * unit_width:(s + 1) * unit_width]).astype(BF) for s in range(tensor)]),
        jnp.stack([dot_tn(branch, active[:, s * unit_width:(s + 1) * unit_width]).astype(BF) for s in range(tensor)]),
    ])
    normed_two_grad = sum(dot_nt(hidden_grad[:, s * unit_width:(s + 1) * unit_width], up_full[s]) for s in range(tensor))
    middle_grad = cotangent + norm_back(normed_two_grad, unit_two, scale_two, gains[1])
    attn_branch = middle_grad.astype(BF)
    ga_full, mlp_grads = k3(geo, attn_branch, grads)

    attended_grad = jnp.dot(ga_full, w_full[3], preferred_element_type=F32).astype(BF)
    project_grad = attend_back(project, segments, log_total, attended_grad)
    dn_part = sum(dot_nt(project_grad[j], w_full[j]) for j in range(3)).astype(BF)
    w_grads = jnp.stack([dot_tn(normed_full, project_grad[j]).astype(BF) for j in range(3)] + [dot_tn(ga_full, attended).astype(BF)])

    query_bias_grad = jnp.sum(project_grad[0].astype(F32), axis=0)
    value_bias_grad = jnp.sum(project_grad[2].astype(F32), axis=0)
    zeros = jnp.zeros((width,), F32)
    dn_total, w_out, small_one = k4_call(geo, dn_part, w_grads, jnp.stack([
        jnp.sum(normed_two_grad * unit_two, axis=0),
        lax.dynamic_update_slice_in_dim(zeros, query_bias_grad, column, 0),
        lax.dynamic_update_slice_in_dim(zeros, value_bias_grad, column, 0),
        jnp.sum(attn_branch.astype(F32), axis=0),
        jnp.sum(normed_two_grad, axis=0),
        jnp.sum(branch.astype(F32), axis=0),
        up_bias_grad[0], up_bias_grad[1], up_bias_grad[2], up_bias_grad[3],
    ]))
    unit_one, scale_one = norm_stats(residual)
    input_grad = middle_grad + norm_back(dn_total, unit_one, scale_one, gains[0])
    late = jnp.stack([jnp.sum(dn_total * unit_one, axis=0), jnp.sum(dn_total, axis=0)])
    late_sum = k5(geo, split_dp(geo, late))
    gain_grad = jnp.stack([late_sum[0], small_one[0]])[None]
    bias_grad = jnp.concatenate([late_sum[1:2], small_one[1:10]], axis=0)[None]
    return (
        output, input_grad, w_out[None, :3], w_out[3].T[None], mlp_grads[0][None], mlp_grads[1].T[None], gain_grad, bias_grad)


def split_dp(geo, rows):
    n, width = rows.shape
    pad = -n % 8
    rows = jnp.pad(rows, ((0, pad), (0, 0)))
    return rows.reshape(n + pad, geo.dp, width // geo.dp).transpose(1, 0, 2)


def k4_call(geo, part, wgrad, small):
    return k4(geo, part, wgrad, split_dp(geo, small))


def k5_body(geo, s_ref, sout, sland, stot, tland, send, recv):
    spot = geo.bind()
    wire = Wire(send, recv)
    greet(spot)
    small = wire.take(geo.dp - 1)
    last = wire.take(geo.tensor - 1)
    for step in range(1, geo.dp):
        to = ring_next(spot.d, step, geo.dp)
        wire.start(small + step - 1, s_ref.at[to], sland.at[step - 1], spot.at_d(to))
    stot[...] = s_ref[spot.d]
    for step in range(1, geo.dp):
        wire.landed(small + step - 1, sland.at[step - 1], spot.at_d(ring_prev(spot.d, step, geo.dp)))
        stot[...] += sland[step - 1]
    for step in range(1, geo.tensor):
        wire.start(last + step - 1, stot, tland.at[step - 1], spot.at_t(ring_next(spot.t, step, geo.tensor)))
    sout[...] = stot[...]
    for step in range(1, geo.tensor):
        wire.landed(last + step - 1, tland.at[step - 1], spot.at_t(ring_prev(spot.t, step, geo.tensor)))
        sout[...] += tland[step - 1]
    wire.drain()


def k5(geo, small):
    sshape = small.shape[1:]
    sems = geo.tensor + geo.dp
    return pl.pallas_call(
        functools.partial(k5_body, geo),
        out_shape=jax.ShapeDtypeStruct(sshape, F32),
        in_specs=[VM],
        out_specs=VM,
        scratch_shapes=[
            pltpu.VMEM((geo.dp - 1,) + sshape, F32),
            pltpu.VMEM(sshape, F32),
            pltpu.VMEM((geo.tensor - 1,) + sshape, F32),
            pltpu.SemaphoreType.DMA((sems,)), pltpu.SemaphoreType.DMA((sems,))],
        compiler_params=pltpu.CompilerParams(collective_id=5, has_side_effects=True),
        name="k5",
    )(small)


def solution(mesh):
    geo = Geometry(mesh.shape["dp"], mesh.shape["tensor"])
    return jax.shard_map(
        functools.partial(per_device, geo),
        mesh=mesh,
        in_specs=(
            P(("dp", "tensor"), None),
            P("dp"),
            P(None, None, "dp", "tensor"),
            P(None, "tensor", "dp"),
            P(None, "dp", "tensor"),
            P(None, "tensor", "dp"),
            P(None, None, "dp"),
            P(None, None, "dp"),
            P(("dp", "tensor"), None),
        ),
        out_specs=(
            P(("dp", "tensor"), None),
            P(("dp", "tensor"), None),
            P(None, None, "dp", "tensor"),
            P(None, "tensor", "dp"),
            P(None, "dp", "tensor"),
            P(None, "tensor", "dp"),
            P(None, None, "dp"),
            P(None, None, "dp"),
        ),
        check_vma=False,
    )
```

time: 848 us -> 513 us (0.60)
  waiting for transfers between devices: 610 us -> 0 us
  Pallas kernels: 0 us -> 333 us
  blocking collectives: 41.5 us -> 0 us
  between operations: 14.7 us -> 1.71 us
  local copies, waits for them, and re-layouts: 35.2 us -> 25.7 us
    pallas_call x0 -> x5, Pallas kernels: none -> 333 us  [the longest x1 123 us: k2(): pl.pallas_call(functools.partial(k2_body, geo), out_shape=(jax.ShapeDtype...]
    reduce_scatter x5 -> x0, waiting for transfers between devices: 255 us -> none  [the longest x1 75 us: layer_forward(): lax.psum_scatter(attn_term(jnp.int32(0), local_rows * lax.axis_size('tens...]
    all_gather x7 -> x0, waiting for transfers between devices: 213 us -> none  [the longest x1 48 us: layer_forward(): normed_two_kept = lax.all_gather(normed_two, 'tensor', axis=0, tiled=True)]
    unnamed x22 -> x0, waiting for transfers between devices: 141 us -> none
    all_gather x3 -> x0, blocking collectives: 28.9 us -> none  [the longest x1 10.3 us: per_device(): lax.all_gather(norm_gains[layer_index], 'dp', axis=1, tiled=True)]
    unnamed x66 -> x68, local copies, waits for them, and re-layouts: 23.8 us -> 8.95 us
    psum x1 -> x0, blocking collectives: 12.6 us -> none  [per_device(): small_sums = lax.psum((stacked[4], stacked[5]), 'tensor')]
    dot_general x26 -> x48, matrix products: 91.4 us -> 89.9 us  [the longest x12 14.6 us: dot_nt(): lax.dot_general(x, w, (((1,), (1,)), ((), ())), preferred_element_type=F32)]
  transfers between devices with their start and end apart: 17 -> 0, of which waited for: 15 -> 0; matrix products, arithmetic and copies ran while one was open for 14% -> 0% of each run, Pallas kernels for 0% -> 0%
where the time goes in v1:
time: 513 us; the launch traced here: 505 us
  Pallas kernels  333 us (65%)
  matrix products  89.9 us (18%)
  other arithmetic  47.3 us (9%)
  local copies, waits for them, and re-layouts  25.7 us (5%)
  loops' own time  7.34 us (1%)
    pallas_call x1, Pallas kernels, k2(): pl.pallas_call(functools.partial(k2_body, geo), out_shape=(jax.ShapeDtype...  123 us
    pallas_call x1, Pallas kernels, k3(): pl.pallas_call(functools.partial(k3_body, geo), out_shape=(jax.ShapeDtype...  118 us
    pallas_call x1, Pallas kernels, k1(): pl.pallas_call(functools.partial(k1_body, geo), out_shape=(jax.ShapeDtype...  42.1 us
    pallas_call x1, Pallas kernels, k4(): pl.pallas_call(functools.partial(k4_body, geo), out_shape=(jax.ShapeDtype...  40.5 us
    dot_general x12, matrix products, dot_nt(): lax.dot_general(x, w, (((1,), (1,)), ((), ())), preferred_element_type=F32)  14.6 us
    dot_general x4, matrix products, block_scores(): jnp.einsum('qhd,khd->hqk', query_rows, key_vecs, preferred_element_type=F32)  12.4 us
    dot_general x2, matrix products, one(): jnp.einsum('qhd,khd->hqk', grad_rows, value_vecs, preferred_element_type=...  11.5 us

profile of v1, /device:TPU:0, one launch (start us, length us, event | category | flops | bytes accessed | tf_op | source)
XLA Modules:
  0.0 505.2 jit_solution(5459337347774920521)
XLA Ops:
  4.6 42.1 %k1.1 = (bf16[1024,1024]{1,0:T(8,128)(2,1)}, bf16[4,1024,256]{2,1,0:T(8,128)(2,1)}, bf16[8,12,128]{2,1,0:T(8,128)(2,1)}) custom-call(bf16[256,1024]{1,0:T(8,128)(2,1)} %x_ref.1, bf16[4,128,256]{2,1,0:T(8,128)(2,1)} %pad_maximum_fusion.4.w_ref, bf16[12,128]{1,0:T(8,128)(2,1)} %pad_maximum_fusion.5.s_ref), custom_call_target="tpu_custom_call" | custom-call | tf_op jit(solution)/shard_map/k1/pallas_call | solution.py:296
  55.0 18.2 %while.27 = (s32[]{:T(128)}, bf16[2,512,256]{2,1,0:T(8,128)(2,1)S(1)}, f32[2,4,512]{2,1,0:T(4,128)S(1)}, s32[2]{0:T(128)S(1)}, s32[1024]{0:T(1024)S(1)}, /*index...) while((s32[]{:T(128)}, bf16[2,512,256]{2,1,0:T(8,128)(2,1)S(1)}, ...), condition=%wide.region_5.6_spmd, body=%wide.region_2.5_spmd.sunk | while | flops 563739136 | bytes 32585916 | solution.py:752
  58.6 2.3 fusion.250
  60.9 2.9 fusion.251
  67.7 2.3 fusion.250
  70.1 2.9 fusion.251
  78.5 123.0 %k2.1 = (f32[256,1024]{1,0:T(8,128)S(1)}, bf16[2,4,1024,1024]{3,2,1,0:T(8,128)(2,1)S(1)}) custom-call(bf16[1024,1024]{1,0:T(8,128)(2,1)S(1)} %convolution_convert_fusion.part, bf16[2,128,1024]{2,1,0:T(8,128)(2,1)S(1)} %pad_maximum_fusion.3.m_ref), custom_call_target="tpu_custom_call" | custom-call | tf_op jit(solution)/shard_map/k2/pallas_call | solution.py:451
  213.7 5.6 %convert_reduce_fusion.1 = (f32[4096]{0:T(1024)}, bf16[256,4096]{1,0:T(8,128)(2,1)S(1)}, bf16[256,4096]{1,0:T(8,128)(2,1)S(1)}) fusion(f32[4096]{0:T(1024)S(1)} %bitcast.354, f32[256,1024]{1,0:T(8,128)S(1)} %fusion.55, f32[256,1024]{1,0:T(8,128)S(1)} %fusion.59, f32[256,1024]{1,0:T(8,128)S(1)} %fusion.63, f32[256,1024]{1,0:T(8,128)S(1)} %fusion.67, ...), kind=kLoop, calls=%fused_computation.59 | loop fusion | flops 32501760 | bytes 12615680 | tf_op jit(solution)/shard_map/reduce_sum | solution.py:826
  238.4 6.8 %pad_maximum_fusion.g_ref = bf16[2,4,1024,1024]{3,2,1,0:T(8,128)(2,1)} fusion(bf16[1,4,1024,1024]{3,2,1,0:T(8,128)(2,1)S(1)} %maximum_bitcast_fusion.1, bf16[1,4,1024,1024]{3,2,1,0:T(8,128)(2,1)S(1)} %maximum_bitcast_fusion), kind=kLoop, calls=%fused_computation.37 | loop fusion | flops 8388608 | bytes 33554432 | tf_op jit(solution)/shard_map/stack | solution.py:827
  245.2 117.8 %k3.1 = (bf16[1024,1024]{1,0:T(8,128)(2,1)}, f32[2,128,1024]{2,1,0:T(8,128)}) custom-call(bf16[256,1024]{1,0:T(8,128)(2,1)} %get-tuple-element.222.ga_ref, bf16[2,4,1024,1024]{3,2,1,0:T(8,128)(2,1)} %pad_maximum_fusion.g_ref), custom_call_target="tpu_custom_call" | custom-call | tf_op jit(solution)/shard_map/k3/pallas_call | solution.py:613
  363.0 3.3 convolution_convert_fusion.5
  366.3 66.8 %while.28 = (s32[]{:T(128)}, f32[1024,4,64]{0,2,1:T(8,128)}, f32[1024,4,64]{0,2,1:T(8,128)}, bf16[2,512,4,64]{1,3,2,0:T(8,128)(2,1)}, s32[2]{0:T(128)S(1)}, /*in...) while((s32[]{:T(128)}, f32[1024,4,64]{0,2,1:T(8,128)}, ...), condition=%wide.region_14.15_spmd.clone, body=%wide.region_12.14_spmd.clone.sunk | while | flops 1376647680 | bytes 131668464 | solution.py:777
  367.9 4.5 fusion.263
  378.4 5.7 %multiply_reduce_fusion.7 = (f32[4,512]{1,0:T(4,128)S(1)}, f32[4,512,1024]{2,1,0:T(8,128)S(1)}) fusion(f32[4,512,1024]{2,1,0:T(8,128)} %fusion.263, f32[4,512]{1,0:T(4,128)S(1)} %dynamic-slice_bitcast_fusion.2, pred[512,1024]{1,0:T(8,128)(4,1)S(1)} %fusion.264, bf16[512,4,64]{0,2,1:T(8,128)(2,1)} %bitcast.336, bf16[1024,4,64]{0,2,1:T(8,128)(2,1)S(1)} %bitcast.334), kind=kOutput, calls=%fused_computation.16.clone.1 | convolution fusion | flops 278919168 | bytes 18104320 | tf_op jit(solution)/shard_map/while/body/eval_jaxpr/qhd,khd->hqk/dot_general | solution.py:768
  384.4 3.7 multiply_convert_fusion.3
  388.1 4.2 fusion.265
  392.3 5.0 fusion.266
  400.9 4.5 fusion.263
  411.5 5.7 %multiply_reduce_fusion.7 = (f32[4,512]{1,0:T(4,128)S(1)}, f32[4,512,1024]{2,1,0:T(8,128)S(1)}) fusion(f32[4,512,1024]{2,1,0:T(8,128)} %fusion.263, f32[4,512]{1,0:T(4,128)S(1)} %dynamic-slice_bitcast_fusion.2, pred[512,1024]{1,0:T(8,128)(4,1)S(1)} %fusion.264, bf16[512,4,64]{0,2,1:T(8,128)(2,1)} %bitcast.336, bf16[1024,4,64]{0,2,1:T(8,128)(2,1)S(1)} %bitcast.334), kind=kOutput, calls=%fused_computation.16.clone.1 | convolution fusion | flops 278919168 | bytes 18104320 | tf_op jit(solution)/shard_map/while/body/eval_jaxpr/qhd,khd->hqk/dot_general | solution.py:768
  417.5 3.7 multiply_convert_fusion.3
  421.1 4.5 fusion.265
  425.6 5.0 fusion.266
  446.5 40.5 %k4.1 = (f32[256,1024]{1,0:T(8,128)S(1)}, f32[4,128,256]{2,1,0:T(8,128)S(1)}, f32[16,128]{1,0:T(8,128)S(1)}) custom-call(bf16[1024,1024]{1,0:T(8,128)(2,1)S(1)} %copy-done, bf16[4,1024,256]{2,1,0:T(8,128)(2,1)S(1)} %pad_maximum_fusion.2.w_ref, f32[8,16,128]{2,1,0:T(8,128)S(1)} %bitcast_bitcast_fusion.s_ref), custom_call_target="tpu_custom_call" | custom-call | tf_op jit(solution)/shard_map/k4/pallas_call | solution.py:700
  493.1 10.0 %k5.1 = f32[8,128]{1,0:T(8,128)} custom-call(f32[8,8,128]{2,1,0:T(8,128)} %fusion.169.s_ref), custom_call_target="tpu_custom_call" | custom-call | tf_op jit(solution)/shard_map/k5/pallas_call | solution.py:899
  (236 shorter events, 90.1 us)
Async XLA Ops:
  46.6 5.5 %copy-start.6 = (bf16[1024,1024]{1,0:T(8,128)(2,1)S(1)}, bf16[1024,1024]{1,0:T(8,128)(2,1)}, u32[]{:S(2)}) copy-start(bf16[1024,1024]{1,0:T(8,128)(2,1)} %get-tuple-element.101) | copy-start | bytes 6291460
  47.6 5.4 %copy-start.27 = (f32[1,8,128]{2,0,1:T(1,128)}, f32[1,8,128]{2,0,1:T(1,128)S(1)}, u32[]{:S(2)}) copy-start(f32[1,8,128]{2,0,1:T(1,128)S(1)} %get-tuple-element.247) | copy-start | bytes 12292
  47.8 5.2 %copy-start.13 = (bf16[4,1024,256]{2,1,0:T(8,128)(2,1)S(1)}, bf16[4,1024,256]{2,1,0:T(8,128)(2,1)}, u32[]{:S(2)}) copy-start(bf16[4,1024,256]{2,1,0:T(8,128)(2,1)} %get-tuple-element.100) | copy-start | bytes 6291460
  73.2 128.2 %copy-start.7 = (bf16[256,1024]{1,0:T(8,128)(2,1)S(1)}, bf16[256,1024]{1,0:T(8,128)(2,1)}, u32[]{:S(2)}) copy-start(bf16[256,1024]{1,0:T(8,128)(2,1)} %x_ref.1) | copy-start | bytes 1572868
  219.3 6.3 %copy-start.9 = (bf16[256,4096]{1,0:T(8,128)(2,1)}, bf16[256,4096]{1,0:T(8,128)(2,1)S(1)}, u32[]{:S(2)}) copy-start(bf16[256,4096]{1,0:T(8,128)(2,1)S(1)} %get-tuple-element.218) | copy-start | bytes 6291460
  378.4 5.8 %slice-start = ((s8[8388608]{0:T(1024)(128)(4,1)}), s8[4194304]{0:T(1024)(128)(4,1)S(1)}, s32[]{:S(2)}) async-start(s8[8388608]{0:T(1024)(128)(4,1)} %bitcast.328), calls=%async_computation | async-start | bytes 8388608 | tf_op jit(solution)/shard_map/while
  378.4 6.0 %slice-start.1 = ((s8[8388608]{0:T(1024)(128)(4,1)}), s8[4194304]{0:T(1024)(128)(4,1)S(1)}, s32[]{:S(2)}) async-start(s8[8388608]{0:T(1024)(128)(4,1)} %bitcast.328), calls=%async_computation.1 | async-start | bytes 8388608 | tf_op jit(solution)/shard_map/while
  388.1 4.2 copy-start.5
  388.1 4.2 copy-start.18
  392.3 5.0 copy-start.1
  392.3 5.0 copy-start.22
  411.5 5.7 %slice-start = ((s8[8388608]{0:T(1024)(128)(4,1)}), s8[4194304]{0:T(1024)(128)(4,1)S(1)}, s32[]{:S(2)}) async-start(s8[8388608]{0:T(1024)(128)(4,1)} %bitcast.328), calls=%async_computation | async-start | bytes 8388608 | tf_op jit(solution)/shard_map/while
  411.5 6.0 %slice-start.1 = ((s8[8388608]{0:T(1024)(128)(4,1)}), s8[4194304]{0:T(1024)(128)(4,1)S(1)}, s32[]{:S(2)}) async-start(s8[8388608]{0:T(1024)(128)(4,1)} %bitcast.328), calls=%async_computation.1 | async-start | bytes 8388608 | tf_op jit(solution)/shard_map/while
  421.1 4.5 copy-start.5
  421.1 4.5 copy-start.18
  425.6 5.0 copy-start.1
  425.6 5.0 copy-start.22
  433.1 3.7 copy-start.4
  444.2 42.8 %copy-start.35 = (f32[256]{0:T(256)S(1)}, f32[256]{0:T(256)}, u32[]{:S(2)}) copy-start(f32[256]{0:T(256)} %get-tuple-element.239) | copy-start | bytes 3076
  444.2 42.8 %copy-start.8 = (bf16[256,1024]{1,0:T(8,128)(2,1)S(1)}, bf16[256,1024]{1,0:T(8,128)(2,1)}, u32[]{:S(2)}) copy-start(bf16[256,1024]{1,0:T(8,128)(2,1)} %x_ref.1) | copy-start | bytes 1572868
  444.2 42.8 %copy-start.28 = (f32[1,8,128]{2,0,1:T(1,128)S(1)}, f32[1,8,128]{2,0,1:T(1,128)}, u32[]{:S(2)}) copy-start(f32[1,8,128]{2,0,1:T(1,128)} %copy-done.27) | copy-start | bytes 12292
  444.2 42.8 %copy-start.30 = (f32[256]{0:T(256)S(1)}, f32[256]{0:T(256)}, u32[]{:S(2)}) copy-start(f32[256]{0:T(256)} %copy-done.29) | copy-start | bytes 3076
  446.5 41.2 %copy-start.11 = (f32[256,1024]{1,0:T(8,128)S(1)}, f32[256,1024]{1,0:T(8,128)}, u32[]{:S(2)}) copy-start(f32[256,1024]{1,0:T(8,128)} %get-tuple-element.223) | copy-start | bytes 3145732
  487.0 3.6 copy-start.17
  (23 other events, 35.6 us)
